TPU v7x, 32 devices: a whole 2x2x4 slice. The times are simulated.
32 devices in a mesh: grp: 4 (over y, x), word: 8 (over z, core).
Axes of the slice: x: 2, y: 2, z: 4, core: 2. Of those that a mesh axis runs over, the one named last changes fastest.
Arguments:
- descriptors: bfloat16 [262144, 128], P(('grp', 'word'))
- word_ids: int32 [262144], P(('grp', 'word')), may hold values from 0 to 1023, as said below
Outputs:
- centroids: bfloat16 [1024, 128], P('word')
- nearest: float32 [262144], P(('grp', 'word'))
Inputs may be any that keep to these rules, and one draw needn't show every extreme that they name: `word_ids`: the word ids of one device's descriptors lie in a window of 64 consecutive ids, counted modulo 1024; every word id from 0 to 1023 occurs at least once.
All inputs are finite; a program needn't handle non-finite values.
Results may differ from a plain program's by a relative error of at most 0.0015.
Values may be sent and summed in bfloat16 or wider, within the bound.
No kernel may reach another device: no remote copies, remote signals or barrier semaphores. Data moves between devices by JAX's collectives and lax.ppermute only.
A program may use at most 64 MiB of HBM per device.

v0:
```python
import jax
import jax.numpy as jnp
from jax import lax
from jax.sharding import PartitionSpec as P

K = 1024


def local_sums(descriptors, word_ids):
    rows = descriptors.shape[0]
    depth = descriptors.shape[1]
    words = K
    block = min(1024, rows)
    xs = descriptors.reshape(rows // block, block, depth)
    idx = word_ids.reshape(rows // block, block)
    table = lax.broadcasted_iota(jnp.int32, (1, words), 1)

    def step(carry, item):
        total, count = carry
        xb, ib = item
        onehot = (ib[:, None] == table).astype(jnp.bfloat16)
        total = total + jnp.einsum("nk,nd->kd", onehot, xb, preferred_element_type=jnp.float32)
        count = count + jnp.sum(onehot.astype(jnp.float32), axis=0)
        return ((total, count), None)

    init = (jnp.zeros((words, depth), jnp.float32), jnp.zeros((words,), jnp.float32))
    (total, count), unused = lax.scan(step, init, (xs, idx))
    return (total, count)


def on_device(descriptors, word_ids):
    total, count = local_sums(descriptors, word_ids)
    xf = descriptors.astype(jnp.float32)
    xnorm = jnp.sum(xf * xf, axis=1)
    depth = descriptors.shape[1]
    start_min = jnp.full(xnorm.shape, jnp.inf, jnp.float32)
    total, count = lax.psum((total, count), ("grp", "word"))
    whole = (total / count[:, None]).astype(jnp.bfloat16)
    pf = whole.astype(jnp.float32)
    cnorm = jnp.sum(pf * pf, axis=1)
    dots = jnp.dot(descriptors, whole.T, preferred_element_type=jnp.float32)
    dist = (xnorm[:, None] - 2.0 * dots + cnorm[None, :]) / depth
    nearest = jnp.minimum(start_min, jnp.min(dist, axis=1))
    owned_rows = whole.shape[0] // lax.axis_size("word")
    begin = lax.axis_index("word") * owned_rows
    cent = lax.dynamic_slice_in_dim(whole, begin, owned_rows, 0)
    return (cent, nearest)


def solution(mesh):
    return jax.shard_map(
        on_device,
        mesh=mesh,
        in_specs=(P(("grp", "word"), None), P(("grp", "word"))),
        out_specs=(P("word", None), P(("grp", "word"))),
        check_vma=False,
    )
```

profile of v0, /device:TPU:0, one launch (start us, length us, event | category | flops | bytes accessed | tf_op | source)
XLA Modules:
  0.0 181.5 jit_solution(9641654276949608156)
XLA Ops:
  7.2 0.8 reshape.15
  8.0 24.5 %while.13 = (s32[]{:T(128)}, f32[1024,128]{1,0:T(8,128)S(1)}, f32[1024]{0:T(1024)S(1)}, s32[8,1024]{1,0:T(8,128)S(1)}, bf16[8,1024,128]{2,1,0:T(8,128)(2,1)}, /*index=5*/s32[]{:T(128)}, s32[]{:T(128)}) while((s32[]{:T(128)}, f32[1024,128]{1,0:T(8,128)S(1)}, f32[1024]{0:T(1024)S(1)}, s32[8,1024]{1,0:T(8,128)S(1)}, ...), condition=%wide.region_2.3_spmd.clone, body=%wide.region_0.2_spmd.clone.sunk | while | flops 273941504 | bytes 1343592 | solution.py:27
  8.0 2.5 %fusion.14 = f32[1024,128]{1,0:T(8,128)S(1)} fusion(s32[1024]{0:T(1024)S(1)} %bitcast.14, f32[1024,128]{1,0:T(8,128)S(1)} %get-tuple-element.108, bf16[8,1024,128]{2,1,0:T(8,128)(2,1)} %get-tuple-element.118, s32[]{:T(128)S(6)} %copy.7, pred[]{:T(512)S(6)} %compare.3), kind=kOutput, calls=%fused_computation.6.clone.1 | convolution fusion | flops 269746176 | bytes 1314821 | tf_op jit(solution)/shard_map/while/body/eval_jaxpr/nk,nd->kd/dot_general | solution.py:22
  10.6 0.5 convert_reduce_fusion.2
  11.1 2.5 %fusion.14 = f32[1024,128]{1,0:T(8,128)S(1)} fusion(s32[1024]{0:T(1024)S(1)} %bitcast.14, f32[1024,128]{1,0:T(8,128)S(1)} %get-tuple-element.108, bf16[8,1024,128]{2,1,0:T(8,128)(2,1)} %get-tuple-element.118, s32[]{:T(128)S(6)} %copy.7, pred[]{:T(512)S(6)} %compare.3), kind=kOutput, calls=%fused_computation.6.clone.1 | convolution fusion | flops 269746176 | bytes 1314821 | tf_op jit(solution)/shard_map/while/body/eval_jaxpr/nk,nd->kd/dot_general | solution.py:22
  13.6 0.5 convert_reduce_fusion.2
  14.2 2.5 %fusion.14 = f32[1024,128]{1,0:T(8,128)S(1)} fusion(s32[1024]{0:T(1024)S(1)} %bitcast.14, f32[1024,128]{1,0:T(8,128)S(1)} %get-tuple-element.108, bf16[8,1024,128]{2,1,0:T(8,128)(2,1)} %get-tuple-element.118, s32[]{:T(128)S(6)} %copy.7, pred[]{:T(512)S(6)} %compare.3), kind=kOutput, calls=%fused_computation.6.clone.1 | convolution fusion | flops 269746176 | bytes 1314821 | tf_op jit(solution)/shard_map/while/body/eval_jaxpr/nk,nd->kd/dot_general | solution.py:22
  16.7 0.5 convert_reduce_fusion.2
  17.2 2.5 %fusion.14 = f32[1024,128]{1,0:T(8,128)S(1)} fusion(s32[1024]{0:T(1024)S(1)} %bitcast.14, f32[1024,128]{1,0:T(8,128)S(1)} %get-tuple-element.108, bf16[8,1024,128]{2,1,0:T(8,128)(2,1)} %get-tuple-element.118, s32[]{:T(128)S(6)} %copy.7, pred[]{:T(512)S(6)} %compare.3), kind=kOutput, calls=%fused_computation.6.clone.1 | convolution fusion | flops 269746176 | bytes 1314821 | tf_op jit(solution)/shard_map/while/body/eval_jaxpr/nk,nd->kd/dot_general | solution.py:22
  19.7 0.5 convert_reduce_fusion.2
  20.3 2.5 %fusion.14 = f32[1024,128]{1,0:T(8,128)S(1)} fusion(s32[1024]{0:T(1024)S(1)} %bitcast.14, f32[1024,128]{1,0:T(8,128)S(1)} %get-tuple-element.108, bf16[8,1024,128]{2,1,0:T(8,128)(2,1)} %get-tuple-element.118, s32[]{:T(128)S(6)} %copy.7, pred[]{:T(512)S(6)} %compare.3), kind=kOutput, calls=%fused_computation.6.clone.1 | convolution fusion | flops 269746176 | bytes 1314821 | tf_op jit(solution)/shard_map/while/body/eval_jaxpr/nk,nd->kd/dot_general | solution.py:22
  22.8 0.5 convert_reduce_fusion.2
  23.3 2.5 %fusion.14 = f32[1024,128]{1,0:T(8,128)S(1)} fusion(s32[1024]{0:T(1024)S(1)} %bitcast.14, f32[1024,128]{1,0:T(8,128)S(1)} %get-tuple-element.108, bf16[8,1024,128]{2,1,0:T(8,128)(2,1)} %get-tuple-element.118, s32[]{:T(128)S(6)} %copy.7, pred[]{:T(512)S(6)} %compare.3), kind=kOutput, calls=%fused_computation.6.clone.1 | convolution fusion | flops 269746176 | bytes 1314821 | tf_op jit(solution)/shard_map/while/body/eval_jaxpr/nk,nd->kd/dot_general | solution.py:22
  25.9 0.5 convert_reduce_fusion.2
  26.4 2.5 %fusion.14 = f32[1024,128]{1,0:T(8,128)S(1)} fusion(s32[1024]{0:T(1024)S(1)} %bitcast.14, f32[1024,128]{1,0:T(8,128)S(1)} %get-tuple-element.108, bf16[8,1024,128]{2,1,0:T(8,128)(2,1)} %get-tuple-element.118, s32[]{:T(128)S(6)} %copy.7, pred[]{:T(512)S(6)} %compare.3), kind=kOutput, calls=%fused_computation.6.clone.1 | convolution fusion | flops 269746176 | bytes 1314821 | tf_op jit(solution)/shard_map/while/body/eval_jaxpr/nk,nd->kd/dot_general | solution.py:22
  28.9 0.5 convert_reduce_fusion.2
  29.5 2.5 %fusion.14 = f32[1024,128]{1,0:T(8,128)S(1)} fusion(s32[1024]{0:T(1024)S(1)} %bitcast.14, f32[1024,128]{1,0:T(8,128)S(1)} %get-tuple-element.108, bf16[8,1024,128]{2,1,0:T(8,128)(2,1)} %get-tuple-element.118, s32[]{:T(128)S(6)} %copy.7, pred[]{:T(512)S(6)} %compare.3), kind=kOutput, calls=%fused_computation.6.clone.1 | convolution fusion | flops 269746176 | bytes 1314821 | tf_op jit(solution)/shard_map/while/body/eval_jaxpr/nk,nd->kd/dot_general | solution.py:22
  32.5 0.8 copy-done.1
  33.3 42.1 %psum.15 = f32[1024]{0:T(1024)S(1)} all-reduce(f32[1024]{0:T(1024)S(1)} %get-tuple-element.36), channel_id=1, replica_groups=mesh['grp'=4,'word'=8] {'grp','word'}, use_global_device_ids=true, to_apply=%region_4.5 | all-reduce | flops 1024 | bytes 8192 | tf_op jit(solution)/shard_map/psum | solution.py:37
  75.4 2.8 %multiply_reduce_fusion.1 = f32[8192]{0:T(1024)S(1)} fusion(bf16[8192,128]{1,0:T(8,128)(2,1)} %bitcast.12), kind=kLoop, calls=%fused_computation.13 | loop fusion | flops 3137536 | bytes 2129920 | tf_op jit(solution)/shard_map/reduce_sum | solution.py:34
  78.2 87.2 %all-reduce.2.cloned.1.call-done = f32[1024,128]{1,0:T(8,128)} async-done(((f32[1024,128]{1,0:T(8,128)}), f32[1024,128]{1,0:T(8,128)}) %all-reduce.2.cloned.1.call-update) | async-done | bytes 524304 | tf_op jit(solution)/shard_map/psum | solution.py:37
  165.4 1.4 multiply_reduce_fusion.2
  166.8 0.6 constant_dynamic-slice_fusion.1
  167.4 7.3 %multiply_reduce_fusion = f32[8192]{0:T(1024)} fusion(f32[1024]{0:T(1024)S(1)} %get-tuple-element.67, f32[8192]{0:T(1024)S(1)} %multiply_reduce_fusion.1, bf16[1024,128]{1,0:T(8,128)(2,1)S(1)} %get-tuple-element.68, bf16[8192,128]{1,0:T(8,128)(2,1)S(1)} %bitcast.13), kind=kOutput, calls=%fused_computation.12 | convolution fusion | flops 2189418496 | bytes 2428928 | tf_op jit(solution)/shard_map/dot_general | solution.py:41
  (24 shorter events, 0.7 us)
Async XLA Ops:
  7.2 158.2 %all-reduce.2.cloned.1.call-start = ((), (), s32[]{:S(2)}) async-start(), calls=%async_computation | async-start | bytes 1048576 | tf_op jit(solution)/shard_map/psum | solution.py:37
  32.5 0.8 copy-start.1
  32.5 134.9 %copy-start = (bf16[8,1024,128]{2,1,0:T(8,128)(2,1)S(1)}, bf16[8,1024,128]{2,1,0:T(8,128)(2,1)}, u32[]{:S(2)}) copy-start(bf16[8,1024,128]{2,1,0:T(8,128)(2,1)} %get-tuple-element.122) | copy-start | bytes 6291460
Sparse Core Ops, SparseCore 0:
  33.5 131.8 all-reduce.1
where the time goes:
time: 182 us
  waiting for transfers between devices  87.2 us (48%)
  blocking collectives  42.1 us (23%)
  matrix products  27.4 us (15%)
  between operations  14.1 us (8%)
  other arithmetic  8.02 us (4%)
  local copies, waits for them, and re-layouts  2.27 us (1%)
    psum x1, waiting for transfers between devices, on_device(): total, count = lax.psum((total, count), ('grp', 'word'))  87.2 us
    psum x1, blocking collectives, on_device(): total, count = lax.psum((total, count), ('grp', 'word'))  42.1 us
    dot_general x8, matrix products, step(): jnp.einsum('nk,nd->kd', onehot, xb, preferred_element_type=jnp.float32)  20.1 us
    dot_general x1, matrix products, on_device(): dots = jnp.dot(descriptors, whole.T, preferred_element_type=jnp.float32)  7.29 us
    reduce_sum x8, other arithmetic, step(): count = count + jnp.sum(onehot.astype(jnp.float32), axis=0)  3.82 us
  transfers between devices with their start and end apart: 1, of which 1 were waited for; matrix products, arithmetic and copies ran while one was open for 2% of the time, Pallas kernels for 0%

commit v1 on v0

--- a/solution.py
+++ b/solution.py
@@ -34,7 +34,7 @@
     xnorm = jnp.sum(xf * xf, axis=1)
     depth = descriptors.shape[1]
     start_min = jnp.full(xnorm.shape, jnp.inf, jnp.float32)
-    total, count = lax.psum((total, count), ("grp", "word"))
+    total, count = lax.psum(lax.psum((total, count), "word"), "grp")
     whole = (total / count[:, None]).astype(jnp.bfloat16)
     pf = whole.astype(jnp.float32)
     cnorm = jnp.sum(pf * pf, axis=1)

time: 182 us -> 157 us (0.86)
  blocking collectives: 42.1 us -> 23.6 us
  waiting for transfers between devices: 87.2 us -> 80.4 us
    psum x1 -> x2, blocking collectives: 42.1 us -> 23.6 us  [on_device(): total, count = lax.psum(lax.psum((total, count), 'word'), 'grp')]
    psum x1 -> x2, waiting for transfers between devices: 87.2 us -> 80.4 us  [on_device(): total, count = lax.psum(lax.psum((total, count), 'word'), 'grp')]
  transfers between devices with their start and end apart: 1 -> 2, of which waited for: 1 -> 2; matrix products, arithmetic and copies ran while one was open for 2% -> 2% of each run, Pallas kernels for 0% -> 0%
where the time goes in v1:
time: 157 us; the launch traced here: 156 us
  waiting for transfers between devices  80.4 us (51%)
  matrix products  27.4 us (17%)
  blocking collectives  23.6 us (15%)
  between operations  14.1 us (9%)
  other arithmetic  8.02 us (5%)
  local copies, waits for them, and re-layouts  2.27 us (1%)
    psum x2, waiting for transfers between devices, on_device(): total, count = lax.psum(lax.psum((total, count), 'word'), 'grp')  80.4 us
    psum x2, blocking collectives, on_device(): total, count = lax.psum(lax.psum((total, count), 'word'), 'grp')  23.6 us
    dot_general x8, matrix products, step(): jnp.einsum('nk,nd->kd', onehot, xb, preferred_element_type=jnp.float32)  20.1 us
    dot_general x1, matrix products, on_device(): dots = jnp.dot(descriptors, whole.T, preferred_element_type=jnp.float32)  7.29 us
    reduce_sum x8, other arithmetic, step(): count = count + jnp.sum(onehot.astype(jnp.float32), axis=0)  3.82 us
  transfers between devices with their start and end apart: 2, of which 2 were waited for; matrix products, arithmetic and copies ran while one was open for 2% of the time, Pallas kernels for 0%

profile of v1, /device:TPU:0, one launch (start us, length us, event | category | flops | bytes accessed | tf_op | source)
XLA Modules:
  0.0 156.3 jit_solution(15688568564056669982)
XLA Ops:
  7.2 0.8 reshape.15
  8.0 24.5 %while.13 = (s32[]{:T(128)}, f32[1024,128]{1,0:T(8,128)S(1)}, f32[1024]{0:T(1024)S(1)}, s32[8,1024]{1,0:T(8,128)S(1)}, bf16[8,1024,128]{2,1,0:T(8,128)(2,1)}, /*index=5*/s32[]{:T(128)}, s32[]{:T(128)}) while((s32[]{:T(128)}, f32[1024,128]{1,0:T(8,128)S(1)}, f32[1024]{0:T(1024)S(1)}, s32[8,1024]{1,0:T(8,128)S(1)}, ...), condition=%wide.region_2.3_spmd.clone, body=%wide.region_0.2_spmd.clone.sunk | while | flops 273941504 | bytes 1343592 | solution.py:27
  8.0 2.5 %fusion.14 = f32[1024,128]{1,0:T(8,128)S(1)} fusion(s32[1024]{0:T(1024)S(1)} %bitcast.14, f32[1024,128]{1,0:T(8,128)S(1)} %get-tuple-element.108, bf16[8,1024,128]{2,1,0:T(8,128)(2,1)} %get-tuple-element.118, s32[]{:T(128)S(6)} %copy.7, pred[]{:T(512)S(6)} %compare.3), kind=kOutput, calls=%fused_computation.6.clone.1 | convolution fusion | flops 269746176 | bytes 1314821 | tf_op jit(solution)/shard_map/while/body/eval_jaxpr/nk,nd->kd/dot_general | solution.py:22
  10.6 0.5 convert_reduce_fusion.2
  11.1 2.5 %fusion.14 = f32[1024,128]{1,0:T(8,128)S(1)} fusion(s32[1024]{0:T(1024)S(1)} %bitcast.14, f32[1024,128]{1,0:T(8,128)S(1)} %get-tuple-element.108, bf16[8,1024,128]{2,1,0:T(8,128)(2,1)} %get-tuple-element.118, s32[]{:T(128)S(6)} %copy.7, pred[]{:T(512)S(6)} %compare.3), kind=kOutput, calls=%fused_computation.6.clone.1 | convolution fusion | flops 269746176 | bytes 1314821 | tf_op jit(solution)/shard_map/while/body/eval_jaxpr/nk,nd->kd/dot_general | solution.py:22
  13.6 0.5 convert_reduce_fusion.2
  14.2 2.5 %fusion.14 = f32[1024,128]{1,0:T(8,128)S(1)} fusion(s32[1024]{0:T(1024)S(1)} %bitcast.14, f32[1024,128]{1,0:T(8,128)S(1)} %get-tuple-element.108, bf16[8,1024,128]{2,1,0:T(8,128)(2,1)} %get-tuple-element.118, s32[]{:T(128)S(6)} %copy.7, pred[]{:T(512)S(6)} %compare.3), kind=kOutput, calls=%fused_computation.6.clone.1 | convolution fusion | flops 269746176 | bytes 1314821 | tf_op jit(solution)/shard_map/while/body/eval_jaxpr/nk,nd->kd/dot_general | solution.py:22
  16.7 0.5 convert_reduce_fusion.2
  17.2 2.5 %fusion.14 = f32[1024,128]{1,0:T(8,128)S(1)} fusion(s32[1024]{0:T(1024)S(1)} %bitcast.14, f32[1024,128]{1,0:T(8,128)S(1)} %get-tuple-element.108, bf16[8,1024,128]{2,1,0:T(8,128)(2,1)} %get-tuple-element.118, s32[]{:T(128)S(6)} %copy.7, pred[]{:T(512)S(6)} %compare.3), kind=kOutput, calls=%fused_computation.6.clone.1 | convolution fusion | flops 269746176 | bytes 1314821 | tf_op jit(solution)/shard_map/while/body/eval_jaxpr/nk,nd->kd/dot_general | solution.py:22
  19.7 0.5 convert_reduce_fusion.2
  20.3 2.5 %fusion.14 = f32[1024,128]{1,0:T(8,128)S(1)} fusion(s32[1024]{0:T(1024)S(1)} %bitcast.14, f32[1024,128]{1,0:T(8,128)S(1)} %get-tuple-element.108, bf16[8,1024,128]{2,1,0:T(8,128)(2,1)} %get-tuple-element.118, s32[]{:T(128)S(6)} %copy.7, pred[]{:T(512)S(6)} %compare.3), kind=kOutput, calls=%fused_computation.6.clone.1 | convolution fusion | flops 269746176 | bytes 1314821 | tf_op jit(solution)/shard_map/while/body/eval_jaxpr/nk,nd->kd/dot_general | solution.py:22
  23.3 2.5 %fusion.14 = f32[1024,128]{1,0:T(8,128)S(1)} fusion(s32[1024]{0:T(1024)S(1)} %bitcast.14, f32[1024,128]{1,0:T(8,128)S(1)} %get-tuple-element.108, bf16[8,1024,128]{2,1,0:T(8,128)(2,1)} %get-tuple-element.118, s32[]{:T(128)S(6)} %copy.7, pred[]{:T(512)S(6)} %compare.3), kind=kOutput, calls=%fused_computation.6.clone.1 | convolution fusion | flops 269746176 | bytes 1314821 | tf_op jit(solution)/shard_map/while/body/eval_jaxpr/nk,nd->kd/dot_general | solution.py:22
  25.9 0.5 convert_reduce_fusion.2
  26.4 2.5 %fusion.14 = f32[1024,128]{1,0:T(8,128)S(1)} fusion(s32[1024]{0:T(1024)S(1)} %bitcast.14, f32[1024,128]{1,0:T(8,128)S(1)} %get-tuple-element.108, bf16[8,1024,128]{2,1,0:T(8,128)(2,1)} %get-tuple-element.118, s32[]{:T(128)S(6)} %copy.7, pred[]{:T(512)S(6)} %compare.3), kind=kOutput, calls=%fused_computation.6.clone.1 | convolution fusion | flops 269746176 | bytes 1314821 | tf_op jit(solution)/shard_map/while/body/eval_jaxpr/nk,nd->kd/dot_general | solution.py:22
  29.5 2.5 %fusion.14 = f32[1024,128]{1,0:T(8,128)S(1)} fusion(s32[1024]{0:T(1024)S(1)} %bitcast.14, f32[1024,128]{1,0:T(8,128)S(1)} %get-tuple-element.108, bf16[8,1024,128]{2,1,0:T(8,128)(2,1)} %get-tuple-element.118, s32[]{:T(128)S(6)} %copy.7, pred[]{:T(512)S(6)} %compare.3), kind=kOutput, calls=%fused_computation.6.clone.1 | convolution fusion | flops 269746176 | bytes 1314821 | tf_op jit(solution)/shard_map/while/body/eval_jaxpr/nk,nd->kd/dot_general | solution.py:22
  32.5 0.8 copy-done.1
  33.4 59.3 %all-reduce.3.cloned.1.call-done = f32[1024,128]{1,0:T(8,128)} async-done(((f32[1024,128]{1,0:T(8,128)}), f32[1024,128]{1,0:T(8,128)}) %all-reduce.3.cloned.1.call-update) | async-done | bytes 524304 | tf_op jit(solution)/shard_map/psum | solution.py:37
  92.7 13.7 %psum.30 = f32[1024]{0:T(1024)S(1)} all-reduce(f32[1024]{0:T(1024)S(1)} %get-tuple-element.36), channel_id=1, replica_groups=mesh['grp'=4,'word'=8] {'word'}, use_global_device_ids=true, to_apply=%region_5.6 | all-reduce | flops 1024 | bytes 8192 | tf_op jit(solution)/shard_map/psum | solution.py:37
  106.4 9.9 %psum.31 = f32[1024]{0:T(1024)S(1)} all-reduce(f32[1024]{0:T(1024)S(1)} %psum.30), channel_id=1, replica_groups=mesh['grp'=4,'word'=8] {'grp'}, use_global_device_ids=true, to_apply=%region_6.7 | all-reduce | flops 1024 | bytes 8192 | tf_op jit(solution)/shard_map/psum | solution.py:37
  116.4 2.7 %multiply_reduce_fusion.1 = f32[8192]{0:T(1024)S(1)} fusion(bf16[8192,128]{1,0:T(8,128)(2,1)} %bitcast.12), kind=kLoop, calls=%fused_computation.13 | loop fusion | flops 3137536 | bytes 2129920 | tf_op jit(solution)/shard_map/reduce_sum | solution.py:34
  119.1 21.1 %all-reduce.5.cloned.1.call-done = f32[1024,128]{1,0:T(8,128)} async-done(((f32[1024,128]{1,0:T(8,128)}), f32[1024,128]{1,0:T(8,128)}) %all-reduce.5.cloned.1.call-update) | async-done | bytes 524304 | tf_op jit(solution)/shard_map/psum | solution.py:37
  140.2 1.4 multiply_reduce_fusion.2
  141.6 0.6 constant_dynamic-slice_fusion.1
  142.2 7.3 %multiply_reduce_fusion = f32[8192]{0:T(1024)} fusion(f32[1024]{0:T(1024)S(1)} %get-tuple-element.67, f32[8192]{0:T(1024)S(1)} %multiply_reduce_fusion.1, bf16[1024,128]{1,0:T(8,128)(2,1)S(1)} %get-tuple-element.68, bf16[8192,128]{1,0:T(8,128)(2,1)S(1)} %bitcast.13), kind=kOutput, calls=%fused_computation.12 | convolution fusion | flops 2189418496 | bytes 2428928 | tf_op jit(solution)/shard_map/dot_general | solution.py:41
  (28 shorter events, 1.7 us)
Async XLA Ops:
  7.2 85.6 %all-reduce.3.cloned.1.call-start = ((), (), s32[]{:S(2)}) async-start(), calls=%async_computation | async-start | bytes 1048576 | tf_op jit(solution)/shard_map/psum | solution.py:37
  32.5 0.8 copy-start.1
  32.5 109.7 %copy-start = (bf16[8,1024,128]{2,1,0:T(8,128)(2,1)S(1)}, bf16[8,1024,128]{2,1,0:T(8,128)(2,1)}, u32[]{:S(2)}) copy-start(bf16[8,1024,128]{2,1,0:T(8,128)(2,1)} %get-tuple-element.123) | copy-start | bytes 6291460
  33.3 106.8 %all-reduce.5.cloned.1.call-start = ((), (), s32[]{:S(2)}) async-start(), calls=%async_computation.1 | async-start | bytes 1048576 | tf_op jit(solution)/shard_map/psum | solution.py:37
Sparse Core Ops, SparseCore 0:
  33.5 59.2 all-reduce.2
  95.7 44.4 all-reduce.4
